TPU v7x, 256 devices: a whole 4x4x8 slice. The times are simulated.
256 devices in a mesh: row: 8 (over z), col: 32 (over y, x, core).
Axes of the slice: x: 4, y: 4, z: 8, core: 2. Of those that a mesh axis runs over, the one named last changes fastest.
Arguments:
- matrix: float32 [16384, 16384], P('row', 'col'), may hold values from -48 to 48, as said below
- pivots: int32 [2, 64], replicated, may hold values from 128 to 16383, as said below
Outputs:
- factored: float32 [16384, 16384], P('row', 'col')
Inputs may be any that keep to these rules, and one draw needn't show every extreme that they name: `pivots`: the 128 entries are distinct global row numbers. `matrix`: the entry of row pivots[c, k] in global column c * 64 + k dominates the other entries of its global column, so that multipliers stay well below one.
All inputs are finite; a program needn't handle non-finite values.
Results may differ from a plain program's by a relative error of at most 0.0002.
Values sent between devices are 32-bit elements; how exact they have to be, the bound alone decides.
A program may use at most 64 MiB of HBM per device.

v0:
```python
import jax
import jax.numpy as jnp
from jax import lax
from jax.sharding import PartitionSpec as P

NB = 64


HIGHEST_PRECISION = lax.Precision.HIGHEST


def from_root(value, axis, source):
    kept = jnp.where(lax.axis_index(axis) == source, value, 0).astype(value.dtype)
    return lax.psum(kept, axis)


def eliminate(panel_t):
    panel_width, row_count = panel_t.shape
    row_ids = jnp.arange(row_count, dtype=jnp.int32)
    col_ids = jnp.arange(panel_width, dtype=jnp.int32)

    def eliminate_step(column, current):
        pivot_line = lax.dynamic_index_in_dim(current, column, 1, keepdims=False)
        pivot_value = lax.dynamic_index_in_dim(pivot_line, column, 0, keepdims=False)
        weight = 1.0 / pivot_value
        column_line = lax.dynamic_index_in_dim(current, column, 0, keepdims=False)
        below_rows = row_ids > column
        multiplier = jnp.where(below_rows, column_line * weight, 0.0)
        later_part = jnp.where(col_ids > column, pivot_line, 0.0)
        current = current - later_part[:, None] * multiplier[None, :]
        return jnp.where(
            (col_ids == column)[:, None] & below_rows[None, :], multiplier[None, :], current
        )

    return lax.fori_loop(0, panel_width, eliminate_step, panel_t)


def solve_rows(top_t, right_side):
    unit_part = jnp.tril(top_t.T, -1) + jnp.eye(top_t.shape[0], dtype=top_t.dtype)
    return lax.linalg.triangular_solve(
        unit_part, right_side, left_side=True, lower=True, unit_diagonal=True
    )


def fetch_rows(local_matrix, global_rows, my_row, grid_rows):
    block_ids = global_rows // NB
    owned = block_ids % grid_rows == my_row
    local_index = block_ids // grid_rows * NB + global_rows % NB
    row_values = jnp.where(owned[:, None], local_matrix[jnp.where(owned, local_index, 0)], 0.0)
    return (row_values, jnp.where(owned, local_index, local_matrix.shape[0]))


def place_rows(local_matrix, local_index, row_values):
    return local_matrix.at[local_index].set(row_values, mode="drop")


def apply_panel(
    local_matrix,
    panel,
    lower_t,
    top_t,
    upper_rows,
    row_blocks,
    col_blocks,
    my_row,
    my_col,
    grid_rows,
    grid_cols,
):
    below_rows = row_blocks > panel
    right_cols = col_blocks > panel
    product = lax.dot_general(
        lower_t,
        upper_rows,
        (((0,), (0,)), ((), ())),
        precision=HIGHEST_PRECISION,
        preferred_element_type=jnp.float32,
    )
    result = jnp.where(
        below_rows[:, None] & right_cols[None, :], local_matrix - product, local_matrix
    )
    col_start = panel // grid_cols * NB
    row_start = panel // grid_rows * NB
    owns_col = my_col == panel % grid_cols
    owns_row = my_row == panel % grid_rows
    col_part = jnp.where(
        below_rows[:, None] & owns_col, lower_t.T, result[:, col_start : col_start + NB]
    )
    result = result.at[:, col_start : col_start + NB].set(col_part)
    row_part = jnp.where(
        right_cols[None, :] & owns_row, upper_rows, result[row_start : row_start + NB]
    )
    result = result.at[row_start : row_start + NB].set(row_part)
    corner = jnp.where(
        owns_row & owns_col, top_t.T, result[row_start : row_start + NB, col_start : col_start + NB]
    )
    return result.at[row_start : row_start + NB, col_start : col_start + NB].set(corner)


def shards(matrix, pivots):
    rows_dev, cols_dev = matrix.shape
    grid_rows = lax.axis_size("row")
    grid_cols = lax.axis_size("col")
    my_row = lax.axis_index("row")
    my_col = lax.axis_index("col")
    row_blocks = jnp.arange(rows_dev, dtype=jnp.int32) // NB * grid_rows + my_row
    col_blocks = jnp.arange(cols_dev, dtype=jnp.int32) // NB * grid_cols + my_col
    local_matrix = matrix
    for panel in range(2):
        top_global = panel * NB + jnp.arange(NB, dtype=jnp.int32)
        pivot_values, pivot_index = fetch_rows(local_matrix, pivots[panel], my_row, grid_rows)
        top_values, top_index = fetch_rows(local_matrix, top_global, my_row, grid_rows)
        new_top, new_pivot = lax.psum((pivot_values, top_values), "row")
        local_matrix = place_rows(
            place_rows(local_matrix, top_index, new_top), pivot_index, new_pivot
        )
        col_start = panel // grid_cols * NB
        panel_t = jnp.concatenate(
            [
                new_top[:, col_start : col_start + NB].T,
                local_matrix[:, col_start : col_start + NB].T,
            ],
            axis=1,
        )
        factored_panel = eliminate(panel_t)
        lower_t, top_t = (
            from_root(factored_panel[:, NB:], "col", panel % grid_cols),
            from_root(factored_panel[:, :NB], "col", panel % grid_cols),
        )
        upper_rows = solve_rows(top_t, new_top)
        local_matrix = apply_panel(
            local_matrix,
            panel,
            lower_t,
            top_t,
            upper_rows,
            row_blocks,
            col_blocks,
            my_row,
            my_col,
            grid_rows,
            grid_cols,
        )
    return local_matrix


def solution(mesh):
    placed = (P("row", "col"), P())
    return jax.shard_map(
        shards, mesh=mesh, in_specs=placed, out_specs=P("row", "col"), check_vma=False
    )
```

profile of v0, /device:TPU:28, one launch (start us, length us, event | category | flops | bytes accessed | tf_op | source)
XLA Modules:
  0.0 980.1 jit_solution(361981040310378852)
XLA Ops:
  6.5 4.7 copy.48
  11.3 2.9 gather_fusion.1
  14.2 2.9 gather_fusion
  17.1 0.7 broadcast_select_fusion.2
  17.8 0.7 broadcast_select_fusion.3
  18.8 0.7 compare_reduce_fusion
  19.5 75.0 %all-reduce.13.cloned.1.call-done = (f32[64,512]{1,0:T(8,128)}, f32[64,512]{1,0:T(8,128)}) async-done(((f32[64,512]{1,0:T(8,128)}, f32[64,512]{1,0:T(8,128)}), (f32[64,512]{1,0:T(8,128)}, f32[64,512]{1,0:T(8,128)})) %all-reduce.13.cloned.1.call-update) | async-done | bytes 262160 | tf_op jit(solution)/shard_map/psum | solution.py:113
  94.5 0.8 slice_bitcast_fusion.3
  95.3 5.3 scatter_fusion
  100.6 5.3 scatter_fusion.1
  105.9 1.3 slice_bitcast_fusion.1
  107.6 133.3 %while.42 = (s32[]{:T(128)}, f32[64,2112]{1,0:T(8,128)S(1)}, s32[]{:T(128)}, f32[1,1]{1,0:T(1,128)}, s32[]{:T(128)}, /*index=5*/s32[]{:T(128)}, s32[]{:T(128)}) while((s32[]{:T(128)}, f32[64,2112]{1,0:T(8,128)S(1)}, s32[]{:T(128)}, f32[1,1]{1,0:T(1,128)}, s32[]{:T(128)}, /*index=5*/s32[]{:T(128)}, s32[]{:T(128)}) %tuple.126), condition=%wide.region_5.6_spmd.clone.clone, body=%wide.region_4.5_spmd.clone.clone.sunk | while | flops 547205 | bytes 2196437 | solution.py:35
  107.6 0.7 dynamic_slice.81
  109.7 0.7 dynamic_slice.81
  111.8 0.7 dynamic_slice.81
  113.9 0.7 dynamic_slice.81
  116.0 0.7 dynamic_slice.81
  118.1 0.7 dynamic_slice.81
  241.3 1.1 slice_select_fusion.1
  242.4 110.9 %psum.59 = f32[64,64]{1,0:T(8,128)S(1)} all-reduce(f32[64,64]{1,0:T(8,128)S(1)} %fusion.17), channel_id=1, replica_groups=mesh['row'=8,'col'=32] {'col'}, use_global_device_ids=true, to_apply=%region_7.8 | all-reduce | flops 4096 | bytes 32768 | tf_op jit(solution)/shard_map/psum | solution.py:14
  353.5 4.9 custom-call.4
  358.8 113.9 %all-reduce.7.cloned.1.call-done = f32[64,2048]{0,1:T(8,128)} async-done(((f32[64,2048]{0,1:T(8,128)}), f32[64,2048]{0,1:T(8,128)}) %all-reduce.7.cloned.1.call-update) | async-done | bytes 524304 | tf_op jit(solution)/shard_map/psum | solution.py:14
  472.7 6.4 subtract_select_fusion.3
  479.1 2.0 copy-done
  481.1 1.0 select_select_fusion.1
  482.2 5.8 scatter.60
  488.0 1.6 constant_dynamic-update-slice_fusion.1
  489.6 2.8 scatter.62
  492.4 2.9 gather_fusion.3
  495.3 2.9 gather_fusion.2
  498.2 0.7 broadcast_select_fusion
  498.9 0.7 broadcast_select_fusion.1
  499.8 75.7 %all-reduce.11.cloned.1.call-done = (f32[64,512]{1,0:T(8,128)}, f32[64,512]{1,0:T(8,128)}) async-done(((f32[64,512]{1,0:T(8,128)}, f32[64,512]{1,0:T(8,128)}), (f32[64,512]{1,0:T(8,128)}, f32[64,512]{1,0:T(8,128)})) %all-reduce.11.cloned.1.call-update) | async-done | bytes 262160 | tf_op jit(solution)/shard_map/psum | solution.py:113
  575.5 0.8 slice_bitcast_fusion.2
  576.2 5.3 scatter_fusion.2
  581.6 5.3 scatter_fusion.3
  586.9 1.3 slice_bitcast_fusion
  588.6 133.3 %while.43 = (s32[]{:T(128)}, f32[64,2112]{1,0:T(8,128)S(1)}, s32[]{:T(128)}, f32[1,1]{1,0:T(1,128)}, s32[]{:T(128)}, /*index=5*/s32[]{:T(128)}, s32[]{:T(128)}) while((s32[]{:T(128)}, f32[64,2112]{1,0:T(8,128)S(1)}, s32[]{:T(128)}, f32[1,1]{1,0:T(1,128)}, s32[]{:T(128)}, /*index=5*/s32[]{:T(128)}, s32[]{:T(128)}) %tuple.129), condition=%wide.region_14.16_spmd.clone.clone, body=%wide.region_13.15_spmd.clone.clone.sunk | while | flops 547205 | bytes 2196437 | solution.py:35
  722.3 1.1 slice_select_fusion
  723.4 111.1 %psum.63 = f32[64,64]{1,0:T(8,128)S(1)} all-reduce(f32[64,64]{1,0:T(8,128)S(1)} %fusion.16), channel_id=1, replica_groups=mesh['row'=8,'col'=32] {'col'}, use_global_device_ids=true, to_apply=%region_16.18 | all-reduce | flops 4096 | bytes 32768 | tf_op jit(solution)/shard_map/psum | solution.py:14
  834.6 4.9 custom-call.5
  839.9 114.0 %all-reduce.9.cloned.1.call-done = f32[64,2048]{0,1:T(8,128)} async-done(((f32[64,2048]{0,1:T(8,128)}), f32[64,2048]{0,1:T(8,128)}) %all-reduce.9.cloned.1.call-update) | async-done | bytes 524304 | tf_op jit(solution)/shard_map/psum | solution.py:14
  953.9 6.4 subtract_select_fusion.2
  960.3 2.0 copy-done.1
  962.3 1.0 select_select_fusion
  963.3 5.8 scatter.65
  969.2 1.6 constant_dynamic-update-slice_fusion
  970.8 2.8 scatter.67
  (943 shorter events, 164.5 us)
Async XLA Ops:
  6.5 4.7 copy-start.6
  6.5 88.0 %all-reduce.13.cloned.1.call-start = ((), (), s32[]{:S(2)}) async-start(), calls=%async_computation.3 | async-start | bytes 524288 | tf_op jit(solution)/shard_map/psum | solution.py:113
  18.6 454.1 %all-reduce.7.cloned.1.call-start = ((), (), s32[]{:S(2)}) async-start(), calls=%async_computation | async-start | bytes 2097152 | tf_op jit(solution)/shard_map/psum | solution.py:14
  240.9 117.5 %copy-start.4 = (f32[64,512]{1,0:T(8,128)S(1)}, f32[64,512]{1,0:T(8,128)}, u32[]{:S(2)}) copy-start(f32[64,512]{1,0:T(8,128)} %get-tuple-element.386) | copy-start | bytes 393220
  353.4 222.1 %all-reduce.11.cloned.1.call-start = ((), (), s32[]{:S(2)}) async-start(), calls=%async_computation.2 | async-start | bytes 524288 | tf_op jit(solution)/shard_map/psum | solution.py:113
  472.7 8.4 copy-start.2
  479.1 2.0 copy-start
  499.7 454.2 %all-reduce.9.cloned.1.call-start = ((), (), s32[]{:S(2)}) async-start(), calls=%async_computation.1 | async-start | bytes 2097152 | tf_op jit(solution)/shard_map/psum | solution.py:14
  721.9 117.6 %copy-start.5 = (f32[64,512]{1,0:T(8,128)S(1)}, f32[64,512]{1,0:T(8,128)}, u32[]{:S(2)}) copy-start(f32[64,512]{1,0:T(8,128)} %get-tuple-element.384) | copy-start | bytes 393220
  953.9 8.4 copy-start.3
  960.3 2.0 copy-start.1
Sparse Core Ops, SparseCore 0:
  18.7 75.7 all-reduce.12
  353.5 119.1 all-reduce.6
  499.8 75.6 all-reduce.10
  834.7 119.1 all-reduce.8
where the time goes:
time: 987 us; the launch traced here: 980 us
  waiting for transfers between devices  379 us (38%)
  blocking collectives  222 us (22%)
  local copies, waits for them, and re-layouts  195 us (20%)
  loops' own time  101 us (10%)
  other arithmetic  56.1 us (6%)
  matrix products  13.5 us (1%)
  between operations  13.4 us (1%)
    psum x2, waiting for transfers between devices, from_root(): return lax.psum(kept, axis)  228 us
    psum x2, blocking collectives, from_root(): return lax.psum(kept, axis)  222 us
    psum x2, waiting for transfers between devices, shards(): new_top, new_pivot = lax.psum((pivot_values, top_values), 'row')  151 us
    another operation x2, loops' own time, eliminate(): return lax.fori_loop(0, panel_width, eliminate_step, panel_t)  101 us
    dynamic_slice x128, local copies, waits for them, and re-layouts, eliminate_step(): lax.dynamic_index_in_dim(pivot_line, column, 0, keepdims=False)  85.8 us
    while x128, local copies, waits for them, and re-layouts  45.2 us
    select_n x128, other arithmetic, eliminate_step(): jnp.where((col_ids == column)[:, None] & below_rows[None, :], multiplier[...  25.8 us
    scatter x4, local copies, waits for them, and re-layouts, place_rows(): return local_matrix.at[local_index].set(row_values, mode='drop')  21.3 us
  transfers between devices with their start and end apart: 4, of which 4 were waited for; matrix products, arithmetic and copies ran while one was open for 1% of the time, Pallas kernels for 0%

commit v1 on v0

v1 whole, which is shorter than its diff:
```python
import jax
import jax.numpy as jnp
from jax import lax
from jax.experimental import pallas as pl
from jax.experimental.pallas import tpu as pltpu
from jax.sharding import PartitionSpec as P

NB = 64
TOP = 2 * NB
SUB = 8
CHUNKS = 8
HIGHEST = lax.Precision.HIGHEST


def dot(a, b):
    return lax.dot_general(
        a, b, (((1,), (0,)), ((), ())), precision=HIGHEST, preferred_element_type=jnp.float32
    )


def factor(a_ref, lu_ref, linv_ref, uinv_ref):
    n = TOP // SUB
    lane = lax.broadcasted_iota(jnp.int32, (SUB, TOP), 1)
    sub = lax.broadcasted_iota(jnp.int32, (SUB, TOP), 0)
    a = [a_ref[SUB * i : SUB * (i + 1), :] for i in range(n)]
    eye = [jnp.where(lane == sub + SUB * i, 1.0, 0.0).astype(jnp.float32) for i in range(n)]
    low = list(eye)
    upp = list(eye)
    weights = jnp.ones((SUB, TOP), jnp.float32)
    for k in range(TOP):
        kb, ks = divmod(k, SUB)
        row = jnp.broadcast_to(a[kb][ks : ks + 1, :], (SUB, TOP))
        low_row = jnp.broadcast_to(low[kb][ks : ks + 1, :], (SUB, TOP))
        weight = 1.0 / jnp.broadcast_to(row[:, k : k + 1], (SUB, TOP))
        weights = jnp.where(lane == k, weight, weights)
        scaled = jnp.where(lane > k, row * weight, 0.0)
        low_scaled = low_row * weight
        for i in range(kb, n):
            column = jnp.broadcast_to(a[i][:, k : k + 1], (SUB, TOP))
            if i == kb:
                column = jnp.where(sub > ks, column, 0.0)
            a[i] = a[i] - column * scaled
            low[i] = low[i] - column * low_scaled
        for i in range(kb + 1):
            column = jnp.broadcast_to(upp[i][:, k : k + 1], (SUB, TOP))
            upp[i] = upp[i] - column * scaled
    for i in range(n):
        part = slice(SUB * i, SUB * (i + 1))
        lu_ref[part, :] = jnp.where(sub + SUB * i > lane, a[i] * weights, a[i])
        linv_ref[part, :] = low[i]
        uinv_ref[part, :] = upp[i] * weights


def finish_kernel(
    where_ref,
    a_ref,
    panel_ref,
    lead_ref,
    new_top_ref,
    old_top_ref,
    old_lead_ref,
    out_ref,
    a_buf,
    p_buf,
    lu,
    linv,
    uinv,
    in_sem,
    panel_sem,
    out_sem,
):
    my_row = lax.axis_index("row")
    my_col = lax.axis_index("col")
    rows = a_buf.shape[0] // CHUNKS
    copies = [
        pltpu.make_async_copy(
            a_ref.at[pl.ds(rows * i, rows)], a_buf.at[pl.ds(rows * i, rows)], in_sem.at[i]
        )
        for i in range(CHUNKS)
    ]
    panel_copy = pltpu.make_async_copy(panel_ref, p_buf, panel_sem)
    panel_copy.start()
    for copy in copies:
        copy.start()
    factor(lead_ref, lu, linv, uinv)
    cols = a_buf.shape[1]
    upper = dot(linv[...], new_top_ref[...])
    solved = dot(uinv[...], upper)
    holds = my_col < 2
    first_cols = lax.broadcasted_iota(jnp.int32, (TOP, cols), 1) < NB
    own = jnp.where(my_col == 0, uinv[:, :NB], uinv[:, NB:])
    own = jnp.concatenate([own, jnp.zeros((TOP, cols - NB), jnp.float32)], axis=1)
    solved = jnp.where(first_cols & holds, -own, solved)
    panel_copy.wait()
    for copy in copies:
        copy.wait()

    def place(k, carry):
        index = where_ref[k]

        @pl.when(index >= 0)
        def _():
            a_buf[pl.ds(index, 1), :] = old_top_ref[pl.ds(k, 1), :]
            p_buf[pl.ds(index, 1), :] = old_lead_ref[pl.ds(k, 1), :]

        return carry

    lax.fori_loop(0, TOP, place, 0)
    dropped = (lax.broadcasted_iota(jnp.int32, (rows, cols), 1) < NB) & holds
    outs = []
    for i in range(CHUNKS):
        part = pl.ds(rows * i, rows)
        kept = jnp.where(dropped, 0.0, a_buf[part, :])
        a_buf[part, :] = kept - dot(p_buf[part, :], solved)
        if i == 0:

            @pl.when(my_row < 2)
            def _():
                half = jnp.where(my_row == 0, upper[:NB], upper[NB:])
                corner = jnp.where(my_row == 0, lu[:NB, :], lu[NB:, :])
                corner = jnp.where(my_col == 0, corner[:, :NB], corner[:, NB:])
                corner = jnp.concatenate(
                    [corner, jnp.zeros((NB, cols - NB), jnp.float32)], axis=1
                )
                a_buf[:NB, :] = jnp.where(first_cols[:NB] & holds, corner, half)

        out = pltpu.make_async_copy(a_buf.at[part], out_ref.at[part], out_sem.at[i])
        out.start()
        outs.append(out)
    for out in outs:
        out.wait()


def finish(matrix, panel, lead, new_top, old_top, old_lead, place_index):
    any_spec = pl.BlockSpec(memory_space=pl.ANY)
    vmem = pl.BlockSpec(memory_space=pltpu.VMEM)
    return pl.pallas_call(
        finish_kernel,
        out_shape=jax.ShapeDtypeStruct(matrix.shape, jnp.float32),
        in_specs=[pl.BlockSpec(memory_space=pltpu.SMEM), any_spec, any_spec] + [vmem] * 4,
        out_specs=any_spec,
        scratch_shapes=[
            pltpu.VMEM(matrix.shape, jnp.float32),
            pltpu.VMEM(panel.shape, jnp.float32),
            pltpu.VMEM((TOP, TOP), jnp.float32),
            pltpu.VMEM((TOP, TOP), jnp.float32),
            pltpu.VMEM((TOP, TOP), jnp.float32),
            pltpu.SemaphoreType.DMA((CHUNKS,)),
            pltpu.SemaphoreType.DMA,
            pltpu.SemaphoreType.DMA((CHUNKS,)),
        ],
        name="finish",
    )(place_index, matrix, panel, lead, new_top, old_top, old_lead)


def shards(matrix, pivots):
    grid_rows = lax.axis_size("row")
    my_row = lax.axis_index("row")
    my_col = lax.axis_index("col")
    pivot = pivots.reshape(-1)
    owned = pivot // NB % grid_rows == my_row
    local = pivot // NB // grid_rows * NB + pivot % NB
    lead_cols = matrix[:, :NB]
    zero = jnp.zeros_like(lead_cols)
    mine = jnp.concatenate(
        [jnp.where(my_col == 0, lead_cols, zero), jnp.where(my_col == 1, lead_cols, zero)], axis=1
    )
    panel = lax.psum(mine, "col")

    def picked(array):
        return jnp.where(owned[:, None], array[jnp.where(owned, local, 0)], 0.0)

    def top_of(array):
        part = array[:NB]
        none = jnp.zeros_like(part)
        return jnp.concatenate(
            [jnp.where(my_row == 0, part, none), jnp.where(my_row == 1, part, none)], axis=0
        )

    new_top, lead, old_top, old_lead = lax.psum(
        (picked(matrix), picked(panel), top_of(matrix), top_of(panel)), "row"
    )
    return finish(
        matrix, panel, lead, new_top, old_top, old_lead, jnp.where(owned, local, -1)
    )


def solution(mesh):
    placed = (P("row", "col"), P())
    return jax.shard_map(
        shards, mesh=mesh, in_specs=placed, out_specs=P("row", "col"), check_vma=False
    )
```

time: 987 us -> 241 us (0.24)
  blocking collectives: 222 us -> 0 us
  waiting for transfers between devices: 379 us -> 188 us
  local copies, waits for them, and re-layouts: 195 us -> 5.09 us
  loops' own time: 101 us -> 0 us
  other arithmetic: 56.1 us -> 6.51 us
  Pallas kernels: 0 us -> 27.5 us
  matrix products: 13.5 us -> 0 us
    psum x2 -> x0, blocking collectives: 222 us -> none  [from_root(): return lax.psum(kept, axis)]
    psum x4 -> x2, waiting for transfers between devices: 379 us -> 188 us  [the longest x1 111 us: shards(): panel = lax.psum(mine, 'col')]
    another operation x2 -> x0, loops' own time: 101 us -> none  [eliminate(): return lax.fori_loop(0, panel_width, eliminate_step, panel_t)]
    dynamic_slice x128 -> x0, local copies, waits for them, and re-layouts: 85.8 us -> none  [eliminate_step(): lax.dynamic_index_in_dim(pivot_line, column, 0, keepdims=False)]
    while x130 -> x0, local copies, waits for them, and re-layouts: 45.9 us -> none
    scatter x8 -> x0, local copies, waits for them, and re-layouts: 38.6 us -> none  [the longest x4 21.3 us: place_rows(): return local_matrix.at[local_index].set(row_values, mode='drop')]
    select_n x269 -> x5, other arithmetic: 36.7 us -> 3.68 us  [the longest x2 1.69 us: top_of(): jnp.where(my_row == 0, part, none)]
    pallas_call x0 -> x1, Pallas kernels: none -> 27.5 us  [finish(): pl.pallas_call(finish_kernel, out_shape=jax.ShapeDtypeStruct(matrix.shape...]
  transfers between devices with their start and end apart: 4 -> 2, of which waited for: 4 -> 2; matrix products, arithmetic and copies ran while one was open for 1% -> 2% of each run, Pallas kernels for 0% -> 0%
where the time goes in v1:
time: 241 us
  waiting for transfers between devices  188 us (78%)
  Pallas kernels  27.5 us (11%)
  between operations  13.4 us (6%)
  other arithmetic  6.51 us (3%)
  local copies, waits for them, and re-layouts  5.09 us (2%)
    psum x1, waiting for transfers between devices, shards(): panel = lax.psum(mine, 'col')  111 us
    psum x1, waiting for transfers between devices, shards(): lax.psum((picked(matrix), picked(panel), top_of(matrix), top_of(panel)),...  77.1 us
    pallas_call x1, Pallas kernels, finish(): pl.pallas_call(finish_kernel, out_shape=jax.ShapeDtypeStruct(matrix.shape...  27.5 us
    gather x2, local copies, waits for them, and re-layouts, picked(): return jnp.where(owned[:, None], array[jnp.where(owned, local, 0)], 0.0)  4.93 us
  transfers between devices with their start and end apart: 2, of which 2 were waited for; matrix products, arithmetic and copies ran while one was open for 2% of the time, Pallas kernels for 0%

profile of v1, /device:TPU:28, one launch (start us, length us, event | category | flops | bytes accessed | tf_op | source)
XLA Modules:
  0.0 240.8 jit_solution(11951726644590428722)
XLA Ops:
  6.5 0.0 copy-start
  6.5 0.0 all-reduce.4.cloned.1.call-start
  6.5 1.4 slice_select_fusion.1
  7.9 1.3 pad_maximum_fusion
  9.2 0.0 all-reduce.4.cloned.1.call-update
  9.2 0.0 all-reduce.6.cloned.1.call-start
  9.3 0.0 copy-done
  9.3 0.1 reshape.195
  9.4 0.1 reshape.194
  9.5 0.6 fusion.2
  10.1 3.1 %gather_fusion.1 = f32[128,512]{1,0:T(8,128)S(1)} fusion(f32[2048,512]{1,0:T(8,128)} %a_ref.1, s32[1024]{0:T(1024)S(1)} %pad_clamp_fusion), kind=kCustom, calls=%fused_computation.1 | custom fusion | bytes 524800 | tf_op jit(solution)/shard_map/gather | solution.py:171
  13.2 0.9 slice_select_fusion.3
  14.1 0.8 pad_maximum_fusion.1
  14.9 111.0 %all-reduce.4.cloned.1.call-done.panel_ref = f32[2048,128]{1,0:T(8,128)} async-done(((f32[2048,128]{1,0:T(8,128)}), f32[2048,128]{1,0:T(8,128)}) %all-reduce.4.cloned.1.call-update) | async-done | bytes 1048592 | tf_op jit(solution)/shard_map/psum | solution.py:168
  125.9 1.9 gather_fusion
  127.7 0.8 slice_select_fusion.5
  128.5 0.7 pad_maximum_fusion.2
  129.2 0.0 all-reduce.6.cloned.1.call-update
  129.2 77.1 %all-reduce.6.cloned.1.call-done = (f32[128,128]{1,0:T(8,128)}, f32[128,512]{1,0:T(8,128)}, f32[128,512]{1,0:T(8,128)}, f32[128,128]{1,0:T(8,128)}) async-done(((f32[128,128]{1,0:T(8,128)}, f32[128,512]{1,0:T(8,128)}, f32[128,512]{1,0:T(8,128)}, f32[128,128]{1,0:T(8,128)}), (f32[128,128]{1,0:T(8,128)}, f32[128,512]{1,0:T(8,128)}, f32[128,512]{1,0:T(8,128)}, ...) | async-done | bytes 655376 | tf_op jit(solution)/shard_map/psum | solution.py:180
  206.4 27.5 %finish.1 = f32[2048,512]{1,0:T(8,128)} custom-call(s32[128]{0:T(128)} %get-tuple-element.9.where_ref, f32[2048,512]{1,0:T(8,128)} %a_ref.1, f32[2048,128]{1,0:T(8,128)} %all-reduce.4.cloned.1.call-done.panel_ref, f32[128,128]{1,0:T(8,128)} %get-tuple-element.5.lead_ref, f32[128,512]{1,0:T(8,128)} %get-tuple-element.6.new_top_ref, ...), custom_call_target="tpu_custom_call" | custom-call | tf_op jit(solution)/shard_map/finish/pallas_call | solution.py:137
  (2 shorter events, 0.0 us)
Async XLA Ops:
  6.5 2.8 %copy-start = (s32[2,64]{1,0:T(2,128)S(1)}, s32[2,64]{1,0:T(2,128)}, u32[]{:S(2)}) copy-start(s32[2,64]{1,0:T(2,128)} %param.3) | copy-start | bytes 1540
  6.5 119.3 %all-reduce.4.cloned.1.call-start = ((), (), s32[]{:S(2)}) async-start(), calls=%async_computation | async-start | bytes 2097152 | tf_op jit(solution)/shard_map/psum | solution.py:168
  9.2 197.1 %all-reduce.6.cloned.1.call-start = ((), (), s32[]{:S(2)}) async-start(), calls=%async_computation.1 | async-start | bytes 1310720 | tf_op jit(solution)/shard_map/psum | solution.py:180
Sparse Core Ops, SparseCore 0:
  10.6 115.2 all-reduce.3
  129.4 76.9 all-reduce.5

commit v2 on v1

--- a/solution.py
+++ b/solution.py
@@ -10,6 +10,7 @@
 SUB = 8
 CHUNKS = 8
 HIGHEST = lax.Precision.HIGHEST
+MESH = pl.DeviceIdType.MESH
 
 
 def dot(a, b):
@@ -153,37 +154,363 @@
     )(place_index, matrix, panel, lead, new_top, old_top, old_lead)
 
 
-def shards(matrix, pivots):
-    grid_rows = lax.axis_size("row")
+def move_kernel(
+    where_ref,
+    a_ref,
+    panel_ref,
+    new_ref,
+    old_ref,
+    lead_ref,
+    old_lead_ref,
+    a_buf,
+    pack,
+    picked,
+    parts,
+    whole,
+    picked_lead,
+    parts_lead,
+    whole_lead,
+    load_sem,
+    slice_send,
+    slice_recv,
+    spread_send,
+    pair_send,
+    pair_recv,
+    part_send,
+    part_recv,
+    top_send,
+    top_recv,
+    whole_send,
+    whole_recv,
+    lead_part_send,
+    lead_part_recv,
+    lead_top_send,
+    lead_top_recv,
+    lead_whole_send,
+    lead_whole_recv,
+):
+    rows_dev = lax.axis_size("row")
+    chips = lax.axis_size("col") // 2
     my_row = lax.axis_index("row")
     my_col = lax.axis_index("col")
+    chip = my_col // 2
+    core = my_col % 2
+    chunk = TOP // rows_dev
+    half_rows = a_buf.shape[0] // 2
+    slice_rows = half_rows // chips
+
+    load = pltpu.make_async_copy(a_ref, a_buf, load_sem)
+    load.start()
+    barrier = pltpu.get_barrier_semaphore()
+    for j in range(1, rows_dev):
+        pl.semaphore_signal(
+            barrier, inc=1, device_id={"row": lax.rem(my_row + j, rows_dev)}, device_id_type=MESH
+        )
+    for j in range(1, chips):
+        pl.semaphore_signal(
+            barrier,
+            inc=1,
+            device_id={"col": lax.rem(chip + j, chips) * 2 + core},
+            device_id_type=MESH,
+        )
+    pl.semaphore_signal(
+        barrier, inc=1, device_id={"col": chip * 2 + 1 - core}, device_id_type=MESH
+    )
+    load.wait()
+
+    def pick(table, target):
+        def body(k, carry):
+            index = where_ref[k]
+            row = table[pl.ds(jnp.maximum(index, 0), 1), :]
+            target[pl.ds(k, 1), :] = jnp.where(index >= 0, row, 0.0)
+            return carry
+
+        lax.fori_loop(0, TOP, body, 0)
+
+    first = lax.broadcasted_iota(jnp.int32, (slice_rows, TOP), 1) < NB
+
+    @pl.when(chip == 0)
+    def _():
+        for s in range(chips):
+            low = a_buf[slice_rows * s : slice_rows * (s + 1), :TOP]
+            high = a_buf[half_rows + slice_rows * s : half_rows + slice_rows * (s + 1), :TOP]
+            at_zero = jnp.where(core == 0, low, high)
+            shifted = jnp.where(core == 0, high, low)
+            pack[core, s] = jnp.where(first, at_zero, pltpu.roll(shifted, NB, 1))
+
+    pick(a_buf, picked)
+    pl.semaphore_wait(barrier, rows_dev - 1 + chips)
+
+    def slice_copy(s, t, send):
+        return pltpu.make_async_remote_copy(
+            src_ref=pack.at[core, s],
+            dst_ref=pack.at[core, s],
+            send_sem=send,
+            recv_sem=slice_recv.at[s],
+            device_id={"col": t * 2 + core},
+            device_id_type=MESH,
+        )
+
+    @pl.when(chip == 0)
+    def _():
+        for s in range(1, chips):
+            slice_copy(s, s, slice_send.at[s]).start()
+
+    def part_copy(j, source, target, send, recv):
+        d = lax.rem(my_row + j, rows_dev)
+        return pltpu.make_async_remote_copy(
+            src_ref=source.at[pl.ds(d * chunk, chunk)],
+            dst_ref=target.at[my_row],
+            send_sem=send.at[j],
+            recv_sem=recv.at[my_row],
+            device_id={"row": d},
+            device_id_type=MESH,
+        )
+
+    def top_copy(d, source, target, send, recv):
+        owner = d * chunk // NB
+        start = d * chunk - owner * NB
+        return pltpu.make_async_remote_copy(
+            src_ref=source.at[pl.ds(start, chunk), :],
+            dst_ref=target.at[d, pl.ds(chunk, chunk)],
+            send_sem=send.at[d],
+            recv_sem=recv,
+            device_id={"row": d},
+            device_id_type=MESH,
+        )
+
+    def whole_copy(j, target, send, recv):
+        return pltpu.make_async_remote_copy(
+            src_ref=target.at[my_row],
+            dst_ref=target.at[my_row],
+            send_sem=send.at[j],
+            recv_sem=recv.at[my_row],
+            device_id={"row": lax.rem(my_row + j, rows_dev)},
+            device_id_type=MESH,
+        )
+
+    def start_rows(source, table, parts, whole, send, recv, t_send, t_recv):
+        for j in range(1, rows_dev):
+            part_copy(j, source, parts, send, recv).start()
+        parts[my_row] = source[pl.ds(pl.multiple_of(my_row * chunk, chunk), chunk), :]
+        for d in range(rows_dev):
+            owner = d * chunk // NB
+            if d == owner:
+
+                @pl.when(my_row == owner)
+                def _():
+                    start = d * chunk - owner * NB
+                    whole[d, chunk:] = table[start : start + chunk, :]
+
+            else:
+
+                @pl.when(my_row == owner)
+                def _():
+                    top_copy(d, table, whole, t_send, t_recv).start()
+
+    def join_rows(source, table, parts, whole, send, recv, t_send, t_recv, w_send, w_recv):
+        for j in range(1, rows_dev):
+            s = lax.rem(my_row + j, rows_dev)
+            pltpu.make_async_remote_copy(
+                src_ref=source.at[pl.ds(0, chunk)],
+                dst_ref=parts.at[s],
+                send_sem=send.at[j],
+                recv_sem=recv.at[s],
+                device_id={"row": s},
+                device_id_type=MESH,
+            ).wait_recv()
+        total = parts[0]
+        for s in range(1, rows_dev):
+            total = total + parts[s]
+        whole[my_row, :chunk] = total
+        for d in range(rows_dev):
+            if d != d * chunk // NB:
+
+                @pl.when(my_row == d)
+                def _():
+                    top_copy(d, table, whole, t_send, t_recv).wait_recv()
+
+        for j in range(1, rows_dev):
+            whole_copy(j, whole, w_send, w_recv).start()
+
+    def end_rows(source, table, parts, whole, new, old, send, recv, t_send, t_recv, w_send, w_recv):
+        for j in range(1, rows_dev):
+            s = lax.rem(my_row + j, rows_dev)
+            pltpu.make_async_remote_copy(
+                src_ref=whole.at[s],
+                dst_ref=whole.at[s],
+                send_sem=w_send.at[j],
+                recv_sem=w_recv.at[s],
+                device_id={"row": s},
+                device_id_type=MESH,
+            ).wait_recv()
+        for d in range(rows_dev):
+            new[chunk * d : chunk * (d + 1), :] = whole[d, :chunk]
+            old[chunk * d : chunk * (d + 1), :] = whole[d, chunk:]
+        for j in range(1, rows_dev):
+            part_copy(j, source, parts, send, recv).wait_send()
+            whole_copy(j, whole, w_send, w_recv).wait_send()
+        for d in range(rows_dev):
+            owner = d * chunk // NB
+            if d != owner:
+
+                @pl.when(my_row == owner)
+                def _():
+                    top_copy(d, table, whole, t_send, t_recv).wait_send()
+
+    main = (part_send, part_recv, top_send, top_recv)
+    start_rows(picked, a_buf, parts, whole, *main)
+
+    @pl.when(chip != 0)
+    def _():
+        slice_copy(chip, chip, slice_send.at[0]).wait_recv()
+
+    for j in range(1, chips):
+        t = lax.rem(chip + j, chips)
+
+        @pl.when(t != 0)
+        def _():
+            slice_copy(chip, t, spread_send.at[j]).start()
+
+    join_rows(picked, a_buf, parts, whole, *main, whole_send, whole_recv)
+
+    groups = min(4, chips)
+    per = chips // groups
+
+    def pair_copy(g, which):
+        return pltpu.make_async_remote_copy(
+            src_ref=pack.at[which, pl.ds(g * per, per)],
+            dst_ref=pack.at[which, pl.ds(g * per, per)],
+            send_sem=pair_send.at[g],
+            recv_sem=pair_recv.at[g],
+            device_id={"col": chip * 2 + 1 - core},
+            device_id_type=MESH,
+        )
+
+    for g in range(groups):
+
+        @pl.when(chip != 0)
+        def _():
+            for s in range(g * per, (g + 1) * per):
+
+                @pl.when(chip != s)
+                def _():
+                    slice_copy(s, chip, slice_send.at[0]).wait_recv()
+
+        pair_copy(g, core).start()
+
+    for g in range(groups):
+        pair_copy(g, 1 - core).wait_recv()
+        for s in range(g * per, (g + 1) * per):
+            zero_pack = pack[0, s]
+            one_pack = pack[1, s]
+            low = slice(slice_rows * s, slice_rows * (s + 1))
+            high = slice(half_rows + slice_rows * s, half_rows + slice_rows * (s + 1))
+            panel_ref[low, :] = jnp.where(first, zero_pack, one_pack)
+            panel_ref[high, :] = pltpu.roll(jnp.where(first, one_pack, zero_pack), NB, 1)
+
+    pick(panel_ref, picked_lead)
+    small = (lead_part_send, lead_part_recv, lead_top_send, lead_top_recv)
+    start_rows(picked_lead, panel_ref, parts_lead, whole_lead, *small)
+    join_rows(
+        picked_lead, panel_ref, parts_lead, whole_lead, *small, lead_whole_send, lead_whole_recv
+    )
+    end_rows(picked, a_buf, parts, whole, new_ref, old_ref, *main, whole_send, whole_recv)
+    end_rows(
+        picked_lead,
+        panel_ref,
+        parts_lead,
+        whole_lead,
+        lead_ref,
+        old_lead_ref,
+        *small,
+        lead_whole_send,
+        lead_whole_recv,
+    )
+
+    @pl.when(chip == 0)
+    def _():
+        for s in range(1, chips):
+            slice_copy(s, s, slice_send.at[s]).wait_send()
+
+    for j in range(1, chips):
+        t = lax.rem(chip + j, chips)
+
+        @pl.when(t != 0)
+        def _():
+            slice_copy(chip, t, spread_send.at[j]).wait_send()
+
+    for g in range(groups):
+        pair_copy(g, core).wait_send()
+
+
+def move(matrix, place_index):
+    rows_dev = lax.axis_size("row")
+    chips = lax.axis_size("col") // 2
+    chunk = TOP // rows_dev
+    rows, cols = matrix.shape
+    dma = pltpu.SemaphoreType.DMA
+    f32 = jnp.float32
+    vmem = pl.BlockSpec(memory_space=pltpu.VMEM)
+
+    def row_sems():
+        return [
+            dma((rows_dev,)),
+            dma((rows_dev,)),
+            dma((rows_dev,)),
+            dma,
+        ]
+
+    return pl.pallas_call(
+        move_kernel,
+        out_shape=[
+            jax.ShapeDtypeStruct((rows, TOP), f32),
+            jax.ShapeDtypeStruct((TOP, cols), f32),
+            jax.ShapeDtypeStruct((TOP, cols), f32),
+            jax.ShapeDtypeStruct((TOP, TOP), f32),
+            jax.ShapeDtypeStruct((TOP, TOP), f32),
+        ],
+        in_specs=[
+            pl.BlockSpec(memory_space=pltpu.SMEM),
+            pl.BlockSpec(memory_space=pl.ANY),
+        ],
+        out_specs=[vmem] * 5,
+        scratch_shapes=[
+            pltpu.VMEM((rows, cols), f32),
+            pltpu.VMEM((2, chips, rows // 2 // chips, TOP), f32),
+            pltpu.VMEM((TOP, cols), f32),
+            pltpu.VMEM((rows_dev, chunk, cols), f32),
+            pltpu.VMEM((rows_dev, 2 * chunk, cols), f32),
+            pltpu.VMEM((TOP, TOP), f32),
+            pltpu.VMEM((rows_dev, chunk, TOP), f32),
+            pltpu.VMEM((rows_dev, 2 * chunk, TOP), f32),
+            dma,
+            dma((chips,)),
+            dma((chips,)),
+            dma((chips,)),
+            dma((4,)),
+            dma((4,)),
+            *row_sems(),
+            dma((rows_dev,)),
+            dma((rows_dev,)),
+            *row_sems(),
+            dma((rows_dev,)),
+            dma((rows_dev,)),
+        ],
+        compiler_params=pltpu.CompilerParams(collective_id=0, has_side_effects=True),
+        name="move",
+    )(place_index, matrix)
+
+
+def shards(matrix, pivots):
+    my_row = lax.axis_index("row")
+    grid_rows = lax.axis_size("row")
     pivot = pivots.reshape(-1)
     owned = pivot // NB % grid_rows == my_row
     local = pivot // NB // grid_rows * NB + pivot % NB
-    lead_cols = matrix[:, :NB]
-    zero = jnp.zeros_like(lead_cols)
-    mine = jnp.concatenate(
-        [jnp.where(my_col == 0, lead_cols, zero), jnp.where(my_col == 1, lead_cols, zero)], axis=1
-    )
-    panel = lax.psum(mine, "col")
-
-    def picked(array):
-        return jnp.where(owned[:, None], array[jnp.where(owned, local, 0)], 0.0)
-
-    def top_of(array):
-        part = array[:NB]
-        none = jnp.zeros_like(part)
-        return jnp.concatenate(
-            [jnp.where(my_row == 0, part, none), jnp.where(my_row == 1, part, none)], axis=0
-        )
-
-    new_top, lead, old_top, old_lead = lax.psum(
-        (picked(matrix), picked(panel), top_of(matrix), top_of(panel)), "row"
-    )
-    return finish(
-        matrix, panel, lead, new_top, old_top, old_lead, jnp.where(owned, local, -1)
-    )
-
+    place_index = jnp.where(owned, local, -1)
+    panel, new_top, old_top, lead, old_lead = move(matrix, place_index)
+    return finish(matrix, panel, lead, new_top, old_top, old_lead, place_index)
 
 def solution(mesh):
     placed = (P("row", "col"), P())

time: 241 us -> 69.8 us (0.29)
  waiting for transfers between devices: 188 us -> 0 us
  Pallas kernels: 27.5 us -> 67.6 us
  between operations: 13.4 us -> 0.01 us
  other arithmetic: 6.51 us -> 0.6 us
  local copies, waits for them, and re-layouts: 5.09 us -> 0.76 us
    psum x2 -> x0, waiting for transfers between devices: 188 us -> none  [the longest x1 111 us: shards(): panel = lax.psum(mine, 'col')]
    pallas_call x0 -> x1, Pallas kernels: none -> 40.2 us  [move(): pl.pallas_call(move_kernel, out_shape=[jax.ShapeDtypeStruct((rows, TOP),...]
    gather x2 -> x0, local copies, waits for them, and re-layouts: 4.93 us -> none  [picked(): return jnp.where(owned[:, None], array[jnp.where(owned, local, 0)], 0.0)]
    select_n x5 -> x1, other arithmetic: 3.68 us -> 0.6 us  [shards(): place_index = jnp.where(owned, local, -1)]
    concatenate x3 -> x0, other arithmetic: 2.83 us -> none  [the longest x2 1.52 us: top_of(): jnp.concatenate([jnp.where(my_row == 0, part, none), jnp.where(my_row ==...]
  transfers between devices with their start and end apart: 2 -> 0, of which waited for: 2 -> 0; matrix products, arithmetic and copies ran while one was open for 2% -> 0% of each run, Pallas kernels for 0% -> 0%
where the time goes in v2:
time: 69.8 us; the launch traced here: 68.9 us
  Pallas kernels  67.6 us (97%)
  local copies, waits for them, and re-layouts  0.76 us (1%)
    pallas_call x1, Pallas kernels, move(): pl.pallas_call(move_kernel, out_shape=[jax.ShapeDtypeStruct((rows, TOP),...  40.2 us
    pallas_call x1, Pallas kernels, finish(): pl.pallas_call(finish_kernel, out_shape=jax.ShapeDtypeStruct(matrix.shape...  27.4 us

profile of v2, /device:TPU:28, one launch (start us, length us, event | category | flops | bytes accessed | tf_op | source)
XLA Modules:
  0.0 68.9 jit_solution(13211738373587866104)
XLA Ops:
  0.0 0.8 %reshape.3 = s32[128]{0:T(128)S(1)} reshape(s32[2,64]{1,0:T(2,128)} %param.3) | data formatting | bytes 1024 | tf_op jit(solution)/shard_map/reshape | solution.py:508
  0.8 0.6 compare_select_fusion.where_ref
  1.4 40.2 %move.1 = (f32[2048,128]{1,0:T(8,128)}, f32[128,512]{1,0:T(8,128)}, f32[128,512]{1,0:T(8,128)}, f32[128,128]{1,0:T(8,128)}, f32[128,128]{1,0:T(8,128)}) custom-call(s32[128]{0:T(128)} %compare_select_fusion.where_ref, f32[2048,512]{1,0:T(8,128)} %a_ref.3), custom_call_target="tpu_custom_call" | custom-call | tf_op jit(solution)/shard_map/move/pallas_call | solution.py:464
  41.5 27.4 %finish.1 = f32[2048,512]{1,0:T(8,128)} custom-call(s32[128]{0:T(128)} %compare_select_fusion.where_ref, f32[2048,512]{1,0:T(8,128)} %a_ref.3, f32[2048,128]{1,0:T(8,128)} %get-tuple-element.10.panel_ref, f32[128,128]{1,0:T(8,128)} %get-tuple-element.11.lead_ref, f32[128,512]{1,0:T(8,128)} %get-tuple-element.12.new_top_ref, ...), custom_call_target="tpu_custom_call" | custom-call | tf_op jit(solution)/shard_map/finish/pallas_call | solution.py:138

commit v3 on v2

--- a/solution.py
+++ b/solution.py
@@ -9,6 +9,7 @@
 TOP = 2 * NB
 SUB = 8
 CHUNKS = 8
+PLACES = 8
 HIGHEST = lax.Precision.HIGHEST
 MESH = pl.DeviceIdType.MESH
 
@@ -17,6 +18,25 @@
     return lax.dot_general(
         a, b, (((1,), (0,)), ((), ())), precision=HIGHEST, preferred_element_type=jnp.float32
     )
+
+
+def halves(x):
+    high = x.astype(jnp.bfloat16)
+    return high, (x - high.astype(jnp.float32)).astype(jnp.bfloat16)
+
+
+def dot_pair(a, b):
+    return lax.dot_general(
+        a, b, (((1,), (0,)), ((), ())), preferred_element_type=jnp.float32
+    )
+
+
+def spread(block, lane):
+    return jnp.broadcast_to(block[:, lane : lane + 1], block.shape)
+
+
+def line(block, row):
+    return jnp.broadcast_to(block[row : row + 1, :], block.shape)
 
 
 def factor(a_ref, lu_ref, linv_ref, uinv_ref):
@@ -24,27 +44,47 @@
     lane = lax.broadcasted_iota(jnp.int32, (SUB, TOP), 1)
     sub = lax.broadcasted_iota(jnp.int32, (SUB, TOP), 0)
     a = [a_ref[SUB * i : SUB * (i + 1), :] for i in range(n)]
-    eye = [jnp.where(lane == sub + SUB * i, 1.0, 0.0).astype(jnp.float32) for i in range(n)]
-    low = list(eye)
-    upp = list(eye)
+    low = [jnp.where(lane == sub + SUB * i, 1.0, 0.0).astype(jnp.float32) for i in range(n)]
+    upp = list(low)
     weights = jnp.ones((SUB, TOP), jnp.float32)
-    for k in range(TOP):
-        kb, ks = divmod(k, SUB)
-        row = jnp.broadcast_to(a[kb][ks : ks + 1, :], (SUB, TOP))
-        low_row = jnp.broadcast_to(low[kb][ks : ks + 1, :], (SUB, TOP))
-        weight = 1.0 / jnp.broadcast_to(row[:, k : k + 1], (SUB, TOP))
-        weights = jnp.where(lane == k, weight, weights)
-        scaled = jnp.where(lane > k, row * weight, 0.0)
-        low_scaled = low_row * weight
-        for i in range(kb, n):
-            column = jnp.broadcast_to(a[i][:, k : k + 1], (SUB, TOP))
-            if i == kb:
-                column = jnp.where(sub > ks, column, 0.0)
-            a[i] = a[i] - column * scaled
-            low[i] = low[i] - column * low_scaled
-        for i in range(kb + 1):
-            column = jnp.broadcast_to(upp[i][:, k : k + 1], (SUB, TOP))
-            upp[i] = upp[i] - column * scaled
+    for b in range(n):
+        first = SUB * b
+        cols = [spread(a[b], first + j) for j in range(SUB)]
+        weight, entry, a_line, low_line = [], [], [], []
+        for k in range(SUB):
+            weight.append(1.0 / line(cols[k], k))
+            weights = jnp.where(lane == first + k, weight[k], weights)
+            entry.append([line(cols[j], k) if j > k else None for j in range(SUB)])
+            a_line.append(jnp.where(lane > first + k, line(a[b], k), 0.0))
+            low_line.append(line(low[b], k))
+            if k < SUB - 1:
+                multiplier = jnp.where(sub > k, cols[k] * weight[k], 0.0)
+                for j in range(k + 1, SUB):
+                    cols[j] = cols[j] - multiplier * entry[k][j]
+                a[b] = a[b] - multiplier * a_line[k]
+                low[b] = low[b] - multiplier * low_line[k]
+
+        def multipliers(cols):
+            cols = list(cols)
+            for k in range(SUB):
+                cols[k] = cols[k] * weight[k]
+                for j in range(k + 1, SUB):
+                    cols[j] = cols[j] - cols[k] * entry[k][j]
+            return cols
+
+        for i in range(b + 1, n):
+            part = multipliers([spread(a[i], first + j) for j in range(SUB)])
+            for k in range(SUB):
+                a[i] = a[i] - part[k] * a_line[k]
+                low[i] = low[i] - part[k] * low_line[k]
+        for i in range(b + 1):
+            if i == b:
+                part = [jnp.where(sub == j, 1.0, 0.0).astype(jnp.float32) for j in range(SUB)]
+            else:
+                part = [spread(upp[i], first + j) for j in range(SUB)]
+            part = multipliers(part)
+            for k in range(SUB):
+                upp[i] = upp[i] - part[k] * a_line[k]
     for i in range(n):
         part = slice(SUB * i, SUB * (i + 1))
         lu_ref[part, :] = jnp.where(sub + SUB * i > lane, a[i] * weights, a[i])
@@ -92,27 +132,33 @@
     own = jnp.where(my_col == 0, uinv[:, :NB], uinv[:, NB:])
     own = jnp.concatenate([own, jnp.zeros((TOP, cols - NB), jnp.float32)], axis=1)
     solved = jnp.where(first_cols & holds, -own, solved)
+    high, rest = halves(solved)
+    twice = jnp.concatenate([high, high], axis=0)
     panel_copy.wait()
     for copy in copies:
         copy.wait()
 
-    def place(k, carry):
-        index = where_ref[k]
-
-        @pl.when(index >= 0)
-        def _():
-            a_buf[pl.ds(index, 1), :] = old_top_ref[pl.ds(k, 1), :]
-            p_buf[pl.ds(index, 1), :] = old_lead_ref[pl.ds(k, 1), :]
+    def place(step, carry):
+        for j in range(PLACES):
+            k = step * PLACES + j
+            index = where_ref[k]
+
+            @pl.when(index >= 0)
+            def _():
+                a_buf[pl.ds(index, 1), :] = old_top_ref[pl.ds(k, 1), :]
+                p_buf[pl.ds(index, 1), :] = old_lead_ref[pl.ds(k, 1), :]
 
         return carry
 
-    lax.fori_loop(0, TOP, place, 0)
+    lax.fori_loop(0, TOP // PLACES, place, 0)
     dropped = (lax.broadcasted_iota(jnp.int32, (rows, cols), 1) < NB) & holds
     outs = []
     for i in range(CHUNKS):
         part = pl.ds(rows * i, rows)
         kept = jnp.where(dropped, 0.0, a_buf[part, :])
-        a_buf[part, :] = kept - dot(p_buf[part, :], solved)
+        left, left_rest = halves(p_buf[part, :])
+        product = dot_pair(jnp.concatenate([left, left_rest], axis=1), twice)
+        a_buf[part, :] = kept - (product + dot_pair(left, rest))
         if i == 0:
 
             @pl.when(my_row < 2)

time: 69.8 us -> 53.4 us (0.77)
  Pallas kernels: 67.6 us -> 51.2 us
    pallas_call x1, Pallas kernels: 27.4 us -> 11.1 us  [finish(): pl.pallas_call(finish_kernel, out_shape=jax.ShapeDtypeStruct(matrix.shape...]
where the time goes in v3:
time: 53.4 us; the launch traced here: 52.6 us
  Pallas kernels  51.2 us (96%)
  local copies, waits for them, and re-layouts  0.76 us (1%)
  other arithmetic  0.6 us (1%)
    pallas_call x1, Pallas kernels, move(): pl.pallas_call(move_kernel, out_shape=[jax.ShapeDtypeStruct((rows, TOP),...  40.2 us
    pallas_call x1, Pallas kernels, finish(): pl.pallas_call(finish_kernel, out_shape=jax.ShapeDtypeStruct(matrix.shape...  11.1 us

profile of v3, /device:TPU:28, one launch (start us, length us, event | category | flops | bytes accessed | tf_op | source)
XLA Modules:
  0.0 52.6 jit_solution(16576001097356382425)
XLA Ops:
  0.0 0.8 %reshape.3 = s32[128]{0:T(128)S(1)} reshape(s32[2,64]{1,0:T(2,128)} %param.3) | data formatting | bytes 1024 | tf_op jit(solution)/shard_map/reshape | solution.py:554
  0.8 0.6 %compare_select_fusion.where_ref = s32[128]{0:T(128)} fusion(s32[128]{0:T(128)S(1)} %reshape.3, s32[]{:T(128)S(6)} %axis_index.15), kind=kLoop, calls=%fused_computation.2 | loop fusion | flops 5376 | bytes 1028 | tf_op jit(solution)/shard_map/jit(_where)/select_n | solution.py:557
  1.4 40.2 %move.1 = (f32[2048,128]{1,0:T(8,128)}, f32[128,512]{1,0:T(8,128)}, f32[128,512]{1,0:T(8,128)}, f32[128,128]{1,0:T(8,128)}, f32[128,128]{1,0:T(8,128)}) custom-call(s32[128]{0:T(128)} %compare_select_fusion.where_ref, f32[2048,512]{1,0:T(8,128)} %a_ref.3), custom_call_target="tpu_custom_call" | custom-call | tf_op jit(solution)/shard_map/move/pallas_call | solution.py:510
  41.5 11.1 %finish.1 = f32[2048,512]{1,0:T(8,128)} custom-call(s32[128]{0:T(128)} %compare_select_fusion.where_ref, f32[2048,512]{1,0:T(8,128)} %a_ref.3, f32[2048,128]{1,0:T(8,128)} %get-tuple-element.10.panel_ref, f32[128,128]{1,0:T(8,128)} %get-tuple-element.11.lead_ref, f32[128,512]{1,0:T(8,128)} %get-tuple-element.12.new_top_ref, ...), custom_call_target="tpu_custom_call" | custom-call | tf_op jit(solution)/shard_map/finish/pallas_call | solution.py:184
